TPU v7x, 128 devices: a whole 4x4x4 slice. The times are simulated.
128 devices in a mesh: tok: 8 (over x, core), voc: 16 (over y, z).
Axes of the slice: x: 4, y: 4, z: 4, core: 2. Of those that a mesh axis runs over, the one named last changes fastest.
Arguments:
- tokens_in: bfloat16 [1024, 4096], P(('tok', 'voc')), may hold values from -36 to 36
- gate_raw: float32 [1024, 8], P(('tok', 'voc')), may hold values from 0.05 to 1
- expert_ids: int32 [1024, 8], P(('tok', 'voc')), may hold values from 0 to 63, all different within a row; in each aligned block of 8 rows (0 to 7, 8 to 15, ...) at most 2 rows name the same one
- w_gate: bfloat16 [4096, 49152], P(None, ('tok', 'voc')), may hold values from -0.09375 to 0.09375
- w_up: bfloat16 [4096, 49152], P(None, ('tok', 'voc')), may hold values from -0.09375 to 0.09375
- w_down: bfloat16 [49152, 4096], P(('tok', 'voc')), may hold values from -0.875 to 0.875
- final_gain: float32 [4096], replicated, may hold values from 0.1 to 1.9
- teacher_head: bfloat16 [4096, 77824], P('tok', 'voc')
- student_hidden: bfloat16 [1024, 4096], P('voc', 'tok'), may hold values from -6 to 6
- student_head: bfloat16 [4096, 77824], P('tok', 'voc')
- sampled_ids: int32 [1024], P('tok'), may hold values from 0 to 77823
- token_weight: float32 [1024], P('tok'), may hold values from 2 to 32
Outputs:
- token_loss: float32 [1024], P('tok')
- hidden_grad: bfloat16 [1024, 4096], P('voc', 'tok')
Inputs may be any that keep to these rules, and one draw needn't show every extreme that they name: `expert_ids`: each row names 8 different experts; in the 8 rows of one device no expert is named by more than 2 rows, a bound that some block reaches.
All inputs are finite; a program needn't handle non-finite values.
Results may differ from a plain program's by a relative error of at most 0.01375.
Values may be sent and summed in bfloat16 or wider, within the bound.
A program may use at most 128 MiB of HBM per device.

v0:
```python
import jax
import jax.numpy as jnp
from jax import lax
from jax.sharding import PartitionSpec as P


def route_tables(expert_ids, gate_raw, experts, capacity):
    rows_here, top_k = expert_ids.shape
    flat_ids = expert_ids.reshape(-1)
    one_hot = (flat_ids[:, None] == jnp.arange(experts, dtype=jnp.int32)[None, :]).astype(jnp.int32)
    earlier = jnp.cumsum(one_hot, axis=0, dtype=jnp.int32) - one_hot
    slot_of = jnp.sum(earlier * one_hot, axis=1, dtype=jnp.int32)
    where_to = (flat_ids * capacity + slot_of).reshape(rows_here, top_k)
    columns = jnp.arange(experts * capacity, dtype=jnp.int32)
    matched = where_to[:, :, None] == columns[None, None, :]
    shares = gate_raw / jnp.sum(gate_raw, axis=1, keepdims=True)
    combine_table = jnp.sum(jnp.where(matched, shares[:, :, None], 0.0), axis=1)
    dispatch_table = jnp.transpose(jnp.any(matched, axis=1)).astype(jnp.bfloat16)
    return (dispatch_table, combine_table)


def per_device(
    tokens_in,
    gate_raw,
    expert_ids,
    w_gate,
    w_up,
    w_down,
    final_gain,
    teacher_head,
    student_hidden,
    student_head,
    sampled_ids,
    token_weight,
):
    tok_count = lax.axis_size("tok")
    voc_count = lax.axis_size("voc")
    experts = tok_count * voc_count // 2
    rows_here, top_k = expert_ids.shape
    model_width = tokens_in.shape[1]
    capacity = max(2, 2 * rows_here * top_k // experts)
    dispatch_table, combine_table = route_tables(expert_ids, gate_raw, experts, capacity)
    dispatched = jnp.dot(dispatch_table, tokens_in, preferred_element_type=jnp.float32).astype(
        jnp.bfloat16
    )
    outgoing = jnp.repeat(dispatched.reshape(experts, capacity, model_width), 2, axis=0)
    arrived = lax.all_to_all(outgoing, ("tok", "voc"), split_axis=0, concat_axis=0, tiled=True)
    expert_rows = arrived.reshape(2 * experts * capacity, model_width)
    gate_part = jnp.dot(expert_rows, w_gate, preferred_element_type=jnp.float32)
    up_part = jnp.dot(expert_rows, w_up, preferred_element_type=jnp.float32)
    hidden_units = (jax.nn.silu(gate_part) * up_part).astype(jnp.bfloat16)
    partial_out = (
        jnp.dot(hidden_units, w_down, preferred_element_type=jnp.float32)
        .astype(jnp.bfloat16)
        .reshape(2 * experts, capacity, model_width)
    )
    returned = lax.all_to_all(partial_out, ("tok", "voc"), split_axis=0, concat_axis=0, tiled=True)
    pair_sum = jnp.sum(
        returned.astype(jnp.float32).reshape(experts, 2, capacity, model_width), axis=1
    ).reshape(experts * capacity, model_width)
    expert_mix = jnp.dot(combine_table, pair_sum, precision=lax.Precision.HIGHEST)
    residual_sum = tokens_in.astype(jnp.float32) + expert_mix
    inverse = lax.rsqrt(jnp.mean(residual_sum * residual_sum, axis=1, keepdims=True) + 1e-06)
    normed = (residual_sum * inverse * final_gain[None, :]).astype(jnp.bfloat16)
    tok_rows = lax.all_gather(normed, "voc", axis=0, tiled=True)
    teacher_cols = lax.all_to_all(tok_rows, "tok", split_axis=1, concat_axis=0, tiled=True)
    student_all = lax.all_gather(student_hidden, "voc", axis=0, tiled=True)
    vocab_local = teacher_head.shape[1]
    rows_piece = teacher_cols
    teacher_logits = lax.psum_scatter(
        jnp.dot(rows_piece, teacher_head, preferred_element_type=jnp.float32).astype(jnp.bfloat16),
        "tok",
        scatter_dimension=0,
        tiled=True,
    ).astype(jnp.float32)
    rows_piece = student_all
    student_logits = lax.psum_scatter(
        jnp.dot(rows_piece, student_head, preferred_element_type=jnp.float32),
        "tok",
        scatter_dimension=0,
        tiled=True,
    )
    differ = student_logits - teacher_logits
    vocab_start = lax.axis_index("voc") * vocab_local
    picked = sampled_ids[:, None] - vocab_start == jnp.arange(vocab_local, dtype=jnp.int32)[None, :]
    picked_s = jnp.sum(jnp.where(picked, student_logits, 0.0), axis=1)
    picked_t = jnp.sum(jnp.where(picked, teacher_logits, 0.0), axis=1)
    local_tmax = jnp.max(teacher_logits, axis=1)
    local_smax = jnp.max(student_logits, axis=1)
    teacher_max, student_max = lax.pmax((local_tmax, local_smax), "voc")
    student_exp = jnp.exp(student_logits - student_max[:, None])
    teacher_sum, student_sum, cross_sum, picked_s, picked_t = lax.psum(
        (
            jnp.sum(jnp.exp(teacher_logits - teacher_max[:, None]), axis=1),
            jnp.sum(student_exp, axis=1),
            jnp.sum(student_exp * differ, axis=1),
            picked_s,
            picked_t,
        ),
        "voc",
    )
    teacher_norm = teacher_max + jnp.log(teacher_sum)
    student_norm = student_max + jnp.log(student_sum)
    expect = cross_sum / student_sum
    token_loss = (
        expect - student_norm + teacher_norm + (picked_s - student_norm) - (picked_t - teacher_norm)
    )
    student_prob = jnp.exp(student_logits - student_norm[:, None])
    logit_grad = (
        token_weight[:, None]
        * (student_prob * (differ - expect[:, None]) + picked.astype(jnp.float32) - student_prob)
    ).astype(jnp.bfloat16)
    grad_terms = lax.dot_general(
        lax.all_gather(logit_grad, "tok", axis=0, tiled=True),
        student_head,
        (((1,), (1,)), ((), ())),
        preferred_element_type=jnp.float32,
    )
    hidden_grad = lax.psum_scatter(
        grad_terms.astype(jnp.bfloat16), "voc", scatter_dimension=0, tiled=True
    )
    return (token_loss, hidden_grad)


def solution(mesh):
    in_specs = (
        P(("tok", "voc"), None),
        P(("tok", "voc"), None),
        P(("tok", "voc"), None),
        P(None, ("tok", "voc")),
        P(None, ("tok", "voc")),
        P(("tok", "voc"), None),
        P(),
        P("tok", "voc"),
        P("voc", "tok"),
        P("tok", "voc"),
        P("tok"),
        P("tok"),
    )
    out_specs = (P("tok"), P("voc", "tok"))
    return jax.shard_map(
        per_device, mesh=mesh, in_specs=in_specs, out_specs=out_specs, check_vma=False
    )
```

profile of v0, /device:TPU:0, one launch (start us, length us, event | category | flops | bytes accessed | tf_op | source)
XLA Modules:
  0.0 612.6 jit_solution(13637765129616562563)
XLA Ops:
  7.2 0.9 eq.20
  8.1 0.1 fusion.12
  8.2 0.1 reduce_window_sum.11
  8.3 0.2 select_reduce_fusion.2
  8.5 0.1 reduce_sum.93
  8.5 0.7 multiply_add_fusion
  9.2 0.1 fusion.11
  9.3 2.3 convolution_convert_fusion.2
  11.6 2.5 reshape.54
  14.2 3.7 broadcast_in_dim.21
  17.9 40.9 %all_to_all.29 = bf16[128,2,4096]{2,1,0:T(2,128)(2,1)} all-to-all(bf16[128,2,4096]{2,1,0:T(2,128)(2,1)S(1)} %bitcast.26), channel_id=1, replica_groups=mesh['tok'=8,'voc'=16] {'tok','voc'}, dimensions={0} | all-to-all | bytes 4194304 | tf_op jit(solution)/shard_map/all_to_all | solution.py:47
  58.8 4.1 reshape.56
  62.9 3.8 fusion.15
  66.7 6.3 %convolution_convert_fusion.1 = bf16[256,4096]{1,0:T(8,128)(2,1)} fusion(bf16[384,4096]{1,0:T(8,128)(2,1)S(1)} %copy-done, bf16[256,4096]{1,0:T(8,128)(2,1)} %reshape.56, bf16[4096,384]{1,0:T(8,128)(2,1)} %param.16, f32[256,384]{1,0:T(8,128)S(1)} %fusion.15), kind=kOutput, calls=%fused_computation.1 | convolution fusion | flops 1612251136 | bytes 10878976 | tf_op jit(solution)/shard_map/dot_general | solution.py:53
  72.9 4.4 reshape.57
  77.3 4.8 all-to-all-start.1
  82.1 0.2 all-gather.6.cloned.1.call-start
  82.4 0.1 reduce_sum.94
  82.5 0.1 broadcast_divide_fusion
  82.6 0.1 select_reduce_fusion.1
  82.7 29.2 %all-to-all-done.1 = bf16[128,2,4096]{2,1,0:T(2,128)(2,1)S(1)} async-done(((bf16[128,2,4096]{2,1,0:T(2,128)(2,1)}), bf16[128,2,4096]{2,1,0:T(2,128)(2,1)S(1)}, u32[]{:S(2)}, u32[]{:S(2)}) %all-to-all-start.1) | async-done | bytes 2097184 | tf_op jit(solution)/shard_map/all_to_all | solution.py:57
  111.9 4.1 convert_reduce_fusion
  116.0 2.7 reshape.60
  118.8 1.2 multiply_reduce_fusion.1
  120.0 0.7 multiply_convert_fusion.1
  120.7 38.7 %all-gather.6.cloned.1.call-done = bf16[128,4096]{1,0:T(8,128)(2,1)} async-done(((bf16[8,4096]{1,0:T(8,128)(2,1)}), bf16[128,4096]{1,0:T(8,128)(2,1)}) %all-gather.6.cloned.1.call-update) | async-done | bytes 1048592 | tf_op jit(solution)/shard_map/all_gather | solution.py:65
  159.5 2.3 copy.18
  161.8 4.3 all-to-all-start.2
  166.1 0.7 all-gather.4.cloned.1.call-update
  166.9 15.1 %all-to-all-done.2 = bf16[128,8,512]{2,0,1:T(8,128)(2,1)S(1)} async-done(((bf16[128,8,512]{2,0,1:T(8,128)(2,1)}), bf16[128,8,512]{2,0,1:T(8,128)(2,1)S(1)}, u32[]{:S(2)}, u32[]{:S(2)}) %all-to-all-start.2) | async-done | bytes 1048608 | tf_op jit(solution)/shard_map/all_to_all | solution.py:66
  182.0 10.2 %convolution_convert_fusion = bf16[1024,4864]{1,0:T(8,128)(2,1)} fusion(bf16[1024,512]{1,0:T(8,128)(2,1)S(1)} %bitcast.27, bf16[512,4864]{1,0:T(8,128)(2,1)} %param.19), kind=kOutput, calls=%fused_computation | convolution fusion | flops 5105254400 | bytes 15990784 | tf_op jit(solution)/shard_map/dot_general | solution.py:71
  192.2 0.0 reduce-scatter.4.cloned.1.call-start
  192.2 19.2 %all-gather.4.cloned.1.call-done = bf16[1024,512]{1,0:T(8,128)(2,1)} async-done(((bf16[64,512]{1,0:T(8,128)(2,1)}), bf16[1024,512]{1,0:T(8,128)(2,1)}) %all-gather.4.cloned.1.call-update) | async-done | bytes 1048592 | tf_op jit(solution)/shard_map/all_gather | solution.py:67
  211.5 12.6 %fusion.14 = f32[1024,4864]{1,0:T(8,128)} fusion(bf16[1024,512]{1,0:T(8,128)(2,1)} %all-gather.4.cloned.1.call-done, bf16[512,4864]{1,0:T(8,128)(2,1)} %param.21), kind=kOutput, calls=%fused_computation.42 | convolution fusion | flops 5100273664 | bytes 25952256 | tf_op jit(solution)/shard_map/dot_general | solution.py:78
  224.1 0.0 all-gather.8.cloned.1.call-start
  224.1 0.6 copy-done.7
  224.7 48.3 %reduce-scatter.6.cloned.1.call-done = bf16[128,4864]{1,0:T(8,128)(2,1)} async-done(((bf16[1024,4864]{1,0:T(8,128)(2,1)}), bf16[128,4864]{1,0:T(8,128)(2,1)}) %reduce-scatter.6.cloned.1.call-update) | async-done | bytes 1245200 | tf_op jit(solution)/shard_map/reduce_scatter | solution.py:70
  273.0 1.5 reduce_max.24
  274.6 107.0 %reduce-scatter.4.cloned.1.call-done = f32[128,4864]{1,0:T(8,128)} async-done(((f32[1024,4864]{1,0:T(8,128)}), f32[128,4864]{1,0:T(8,128)}) %reduce-scatter.4.cloned.1.call-update) | async-done | bytes 2490384 | tf_op jit(solution)/shard_map/reduce_scatter | solution.py:77
  381.6 2.0 reduce_max.23
  383.7 41.3 %all-reduce.1 = (f32[128]{0:T(128)S(1)}, f32[128]{0:T(128)S(1)}) all-reduce(f32[128]{0:T(128)S(1)} %reduce_max.23, bf16[128]{0:T(256)(128)(2,1)S(1)} %reduce_max.24), channel_id=1, replica_groups=mesh['tok'=8,'voc'=16] {'voc'}, use_global_device_ids=true, to_apply=%region_2.3 | all-reduce | flops 256 | bytes 1792 | tf_op jit(solution)/shard_map/pmax | solution.py:90
  425.0 3.6 multiply_reduce_fusion
  428.5 35.5 %all-reduce = (f32[128]{0:T(128)S(1)}, f32[128]{0:T(128)S(1)}, f32[128]{0:T(128)S(1)}, f32[128]{0:T(128)S(1)}, f32[128]{0:T(128)S(1)}) all-reduce(f32[128]{0:T(128)S(1)} %get-tuple-element.5, f32[128]{0:T(128)S(1)} %get-tuple-element.4, f32[128]{0:T(128)S(1)} %get-tuple-element.3, ...), channel_id=1, replica_groups=mesh['tok'=8,'voc'=16] {'voc'}, use_global_device_ids=true, to_apply=%region_22.23 | all-reduce | flops 640 | bytes 5120 | tf_op jit(solution)/shard_map/psum | solution.py:92
  464.0 0.5 subtract_subtract_fusion
  464.5 3.5 multiply_convert_fusion
  468.1 51.9 %all-gather.8.cloned.1.call-done = bf16[1024,4864]{1,0:T(8,128)(2,1)} async-done(((bf16[128,4864]{1,0:T(8,128)(2,1)}), bf16[1024,4864]{1,0:T(8,128)(2,1)}) %all-gather.8.cloned.1.call-update) | async-done | bytes 9961488 | tf_op jit(solution)/shard_map/all_gather | solution.py:114
  520.0 11.1 %convolution_convert_fusion.3 = bf16[1024,512]{1,0:T(8,128)(2,1)} fusion(bf16[1024,4864]{1,0:T(8,128)(2,1)} %all-gather.8.cloned.1.call-done, bf16[512,4864]{1,0:T(8,128)(2,1)} %param.21), kind=kOutput, calls=%fused_computation.17 | convolution fusion | flops 5100797952 | bytes 15990784 | tf_op jit(solution)/shard_map/dot_general | solution.py:113
  531.2 74.6 %reduce-scatter.8.cloned.1.call-done = bf16[64,512]{1,0:T(8,128)(2,1)} async-done(((bf16[1024,512]{1,0:T(8,128)(2,1)}), bf16[64,512]{1,0:T(8,128)(2,1)}) %reduce-scatter.8.cloned.1.call-update) | async-done | bytes 65552 | tf_op jit(solution)/shard_map/reduce_scatter | solution.py:119
  (25 shorter events, 0.2 us)
Async XLA Ops:
  7.2 59.5 %copy-start = (bf16[384,4096]{1,0:T(8,128)(2,1)S(1)}, bf16[384,4096]{1,0:T(8,128)(2,1)}, u32[]{:S(2)}) copy-start(bf16[384,4096]{1,0:T(8,128)(2,1)} %param.17) | copy-start | bytes 9437188
  77.3 5.0 copy-start.4
  77.3 34.6 %all-to-all-start.1 = ((bf16[128,2,4096]{2,1,0:T(2,128)(2,1)}), bf16[128,2,4096]{2,1,0:T(2,128)(2,1)S(1)}, u32[]{:S(2)}, u32[]{:S(2)}) async-start(bf16[128,2,4096]{2,1,0:T(2,128)(2,1)} %reshape.57), calls=%async_computation.2 | async-start | bytes 4194304 | tf_op jit(solution)/shard_map/all_to_all | solution.py:57
  82.1 77.4 %all-gather.6.cloned.1.call-start = ((), (), s32[]{:S(2)}) async-start(), calls=%async_computation.8 | async-start | bytes 1114112 | tf_op jit(solution)/shard_map/all_gather | solution.py:65
  116.0 2.7 copy-start.3
  116.0 4.0 copy-start.5
  161.8 20.2 %all-to-all-start.2 = ((bf16[128,8,512]{2,0,1:T(8,128)(2,1)}), bf16[128,8,512]{2,0,1:T(8,128)(2,1)S(1)}, u32[]{:S(2)}, u32[]{:S(2)}) async-start(bf16[128,8,512]{2,0,1:T(8,128)(2,1)} %bitcast.25), calls=%async_computation.3 | async-start | bytes 2097152 | tf_op jit(solution)/shard_map/all_to_all | solution.py:66
  166.1 45.4 %all-gather.4.cloned.1.call-start = ((), (), s32[]{:S(2)}) async-start(), calls=%async_computation.6 | async-start | bytes 1114112 | tf_op jit(solution)/shard_map/all_gather | solution.py:67
  166.8 106.2 %reduce-scatter.6.cloned.1.call-start = ((), (), s32[]{:S(2)}) async-start(), calls=%async_computation.9 | async-start | bytes 11206656 | tf_op jit(solution)/shard_map/reduce_scatter | solution.py:70
  192.2 189.4 %reduce-scatter.4.cloned.1.call-start = ((), (), s32[]{:S(2)}) async-start(), calls=%async_computation.7 | async-start | bytes 22413312 | tf_op jit(solution)/shard_map/reduce_scatter | solution.py:77
  224.0 0.7 copy-start.7
  224.1 296.0 %all-gather.8.cloned.1.call-start = ((), (), s32[]{:S(2)}) async-start(), calls=%async_computation.10 | async-start | bytes 11206656 | tf_op jit(solution)/shard_map/all_gather | solution.py:114
  381.6 43.4 %copy-start.2 = (f32[128,4864]{1,0:T(8,128)S(1)}, f32[128,4864]{1,0:T(8,128)}, u32[]{:S(2)}) copy-start(f32[128,4864]{1,0:T(8,128)} %reduce-scatter.4.cloned.1.call-done) | copy-start | bytes 7471108
  383.7 80.9 %copy-start.6 = (f32[128]{0:T(128)S(1)}, f32[128]{0:T(128)}, u32[]{:S(2)}) copy-start(f32[128]{0:T(128)} %param.23) | copy-start | bytes 1540
  468.1 137.7 %reduce-scatter.8.cloned.1.call-start = ((), (), s32[]{:S(2)}) async-start(), calls=%async_computation.11 | async-start | bytes 1114112 | tf_op jit(solution)/shard_map/reduce_scatter | solution.py:119
  520.0 85.7 %copy-start.1 = (bf16[384,4096]{1,0:T(8,128)(2,1)S(1)}, bf16[384,4096]{1,0:T(8,128)(2,1)}, u32[]{:S(2)}) copy-start(bf16[384,4096]{1,0:T(8,128)(2,1)} %param.17) | copy-start | bytes 9437188
Sparse Core Ops, SparseCore 0:
  120.9 38.5 all-gather.5
  169.0 42.4 all-gather.3
  213.9 59.1 reduce-scatter.5
  275.3 106.2 reduce-scatter.3
  468.2 51.7 all-gather.7
  531.3 74.4 reduce-scatter.7
where the time goes:
time: 613 us
  waiting for transfers between devices  385 us (63%)
  blocking collectives  118 us (19%)
  matrix products  47.4 us (8%)
  local copies, waits for them, and re-layouts  21.4 us (3%)
  other arithmetic  17.5 us (3%)
  between operations  14.2 us (2%)
  starting transfers between devices  9.46 us (2%)
    reduce_scatter x1, waiting for transfers between devices, per_device(): lax.psum_scatter(jnp.dot(rows_piece, student_head, preferred_element_type...  107 us
    reduce_scatter x1, waiting for transfers between devices, per_device(): lax.psum_scatter(grad_terms.astype(jnp.bfloat16), 'voc', scatter_dimensio...  74.6 us
    all_gather x1, waiting for transfers between devices, per_device(): lax.all_gather(logit_grad, 'tok', axis=0, tiled=True)  51.9 us
    reduce_scatter x1, waiting for transfers between devices, per_device(): lax.psum_scatter(jnp.dot(rows_piece, teacher_head, preferred_element_type...  48.3 us
    pmax x1, blocking collectives, per_device(): teacher_max, student_max = lax.pmax((local_tmax, local_smax), 'voc')  41.3 us
    all_to_all x1, blocking collectives, per_device(): lax.all_to_all(outgoing, ('tok', 'voc'), split_axis=0, concat_axis=0, til...  40.9 us
    all_gather x1, waiting for transfers between devices, per_device(): tok_rows = lax.all_gather(normed, 'voc', axis=0, tiled=True)  38.7 us
    psum x1, blocking collectives, per_device(): lax.psum((jnp.sum(jnp.exp(teacher_logits - teacher_max[:, None]), axis=1)...  35.5 us
  transfers between devices with their start and end apart: 8, of which 8 were waited for; matrix products, arithmetic and copies ran while one was open for 4% of the time, Pallas kernels for 0%

commit v1 on v0

--- a/solution.py
+++ b/solution.py
@@ -62,7 +62,9 @@
     residual_sum = tokens_in.astype(jnp.float32) + expert_mix
     inverse = lax.rsqrt(jnp.mean(residual_sum * residual_sum, axis=1, keepdims=True) + 1e-06)
     normed = (residual_sum * inverse * final_gain[None, :]).astype(jnp.bfloat16)
-    tok_rows = lax.all_gather(normed, "voc", axis=0, tiled=True)
+    tok_rows = jnp.concatenate(
+        lax.all_to_all(jnp.stack([normed] * lax.axis_size("voc")), "voc", 0, 0), axis=0
+    )
     teacher_cols = lax.all_to_all(tok_rows, "tok", split_axis=1, concat_axis=0, tiled=True)
     student_all = lax.all_gather(student_hidden, "voc", axis=0, tiled=True)
     vocab_local = teacher_head.shape[1]

time: 613 us -> 569 us (0.928)
  waiting for transfers between devices: 385 us -> 322 us
  blocking collectives: 118 us -> 138 us
    all_gather x1 -> x0, waiting for transfers between devices: 38.7 us -> none  [per_device(): tok_rows = lax.all_gather(normed, 'voc', axis=0, tiled=True)]
    reduce_scatter x1, waiting for transfers between devices: 48.3 us -> 25.1 us  [per_device(): lax.psum_scatter(jnp.dot(rows_piece, teacher_head, preferred_element_type...]
    all_to_all x0 -> x1, blocking collectives: none -> 19.9 us  [per_device(): lax.all_to_all(jnp.stack([normed] * lax.axis_size('voc')), 'voc', 0, 0)]
  transfers between devices with their start and end apart: 8 -> 7, of which waited for: 8 -> 7; matrix products, arithmetic and copies ran while one was open for 4% -> 4% of each run, Pallas kernels for 0% -> 0%
where the time goes in v1:
time: 569 us
  waiting for transfers between devices  322 us (57%)
  blocking collectives  138 us (24%)
  matrix products  47.3 us (8%)
  local copies, waits for them, and re-layouts  20.9 us (4%)
  other arithmetic  16.9 us (3%)
  between operations  15.8 us (3%)
  starting transfers between devices  8.73 us (2%)
    reduce_scatter x1, waiting for transfers between devices, per_device(): lax.psum_scatter(jnp.dot(rows_piece, student_head, preferred_element_type...  107 us
    reduce_scatter x1, waiting for transfers between devices, per_device(): lax.psum_scatter(grad_terms.astype(jnp.bfloat16), 'voc', scatter_dimensio...  74.6 us
    all_gather x1, waiting for transfers between devices, per_device(): lax.all_gather(logit_grad, 'tok', axis=0, tiled=True)  51.8 us
    pmax x1, blocking collectives, per_device(): teacher_max, student_max = lax.pmax((local_tmax, local_smax), 'voc')  41.3 us
    all_to_all x1, blocking collectives, per_device(): lax.all_to_all(outgoing, ('tok', 'voc'), split_axis=0, concat_axis=0, til...  40.9 us
    psum x1, blocking collectives, per_device(): lax.psum((jnp.sum(jnp.exp(teacher_logits - teacher_max[:, None]), axis=1)...  35.5 us
    all_to_all x1, waiting for transfers between devices, per_device(): lax.all_to_all(partial_out, ('tok', 'voc'), split_axis=0, concat_axis=0,...  29.3 us
    reduce_scatter x1, waiting for transfers between devices, per_device(): lax.psum_scatter(jnp.dot(rows_piece, teacher_head, preferred_element_type...  25.1 us
  transfers between devices with their start and end apart: 7, of which 7 were waited for; matrix products, arithmetic and copies ran while one was open for 4% of the time, Pallas kernels for 0%

profile of v1, /device:TPU:0, one launch (start us, length us, event | category | flops | bytes accessed | tf_op | source)
XLA Modules:
  0.0 568.7 jit_solution(10436294012160777815)
XLA Ops:
  8.0 0.9 eq.20
  8.9 0.1 fusion.12
  9.0 0.1 reduce_window_sum.11
  9.1 0.2 select_reduce_fusion.2
  9.3 0.1 reduce_sum.93
  9.4 0.7 multiply_add_fusion
  10.1 0.1 fusion.11
  10.2 2.3 convolution_convert_fusion.2
  12.5 2.5 reshape.58
  15.0 3.7 broadcast_in_dim.21
  18.7 40.9 %all_to_all.34 = bf16[128,2,4096]{2,1,0:T(2,128)(2,1)} all-to-all(bf16[128,2,4096]{2,1,0:T(2,128)(2,1)S(1)} %bitcast.25), channel_id=1, replica_groups=mesh['tok'=8,'voc'=16] {'tok','voc'}, dimensions={0} | all-to-all | bytes 4194304 | tf_op jit(solution)/shard_map/all_to_all | solution.py:47
  59.6 4.1 reshape.60
  63.7 3.8 fusion.15
  67.5 6.3 %convolution_convert_fusion.1 = bf16[256,4096]{1,0:T(8,128)(2,1)} fusion(bf16[384,4096]{1,0:T(8,128)(2,1)S(1)} %copy-done, bf16[256,4096]{1,0:T(8,128)(2,1)} %reshape.60, bf16[4096,384]{1,0:T(8,128)(2,1)} %param.16, f32[256,384]{1,0:T(8,128)S(1)} %fusion.15), kind=kOutput, calls=%fused_computation.1 | convolution fusion | flops 1612251136 | bytes 10878976 | tf_op jit(solution)/shard_map/dot_general | solution.py:53
  73.8 4.4 reshape.61
  78.2 5.0 all-to-all-start.1
  83.2 0.1 reduce_sum.94
  83.3 0.1 broadcast_divide_fusion
  83.3 0.1 select_reduce_fusion.1
  83.4 29.3 %all-to-all-done.1 = bf16[128,2,4096]{2,1,0:T(2,128)(2,1)S(1)} async-done(((bf16[128,2,4096]{2,1,0:T(2,128)(2,1)}), bf16[128,2,4096]{2,1,0:T(2,128)(2,1)S(1)}, u32[]{:S(2)}, u32[]{:S(2)}) %all-to-all-start.1) | async-done | bytes 2097184 | tf_op jit(solution)/shard_map/all_to_all | solution.py:57
  112.7 4.1 convert_reduce_fusion
  116.9 2.7 reshape.64
  119.6 1.2 multiply_reduce_fusion.1
  120.8 0.1 multiply_convert_fusion.1
  120.9 0.1 stack.2
  121.0 19.9 %all_to_all.35 = bf16[16,8,4096]{2,1,0:T(8,128)(2,1)S(1)} all-to-all(bf16[16,8,4096]{2,1,0:T(8,128)(2,1)S(1)} %stack.2), channel_id=1, replica_groups=mesh['tok'=8,'voc'=16] {'voc'}, dimensions={0} | all-to-all | bytes 2097152 | tf_op jit(solution)/shard_map/all_to_all | solution.py:66
  140.9 0.4 copy.17
  141.3 1.3 copy.16
  142.6 3.6 all-to-all-start.3
  146.2 0.7 all-gather.3.cloned.1.call-update
  147.0 15.1 %all-to-all-done.3 = bf16[128,8,512]{2,0,1:T(8,128)(2,1)S(1)} async-done(((bf16[128,8,512]{2,0,1:T(8,128)(2,1)}), bf16[128,8,512]{2,0,1:T(8,128)(2,1)S(1)}, u32[]{:S(2)}, u32[]{:S(2)}) %all-to-all-start.3) | async-done | bytes 1048608 | tf_op jit(solution)/shard_map/all_to_all | solution.py:68
  162.1 10.2 %convolution_convert_fusion = bf16[1024,4864]{1,0:T(8,128)(2,1)} fusion(bf16[1024,512]{1,0:T(8,128)(2,1)S(1)} %bitcast.28, bf16[512,4864]{1,0:T(8,128)(2,1)} %param.19), kind=kOutput, calls=%fused_computation | convolution fusion | flops 5105254400 | bytes 15990784 | tf_op jit(solution)/shard_map/dot_general | solution.py:73
  172.3 0.0 reduce-scatter.4.cloned.1.call-start
  172.3 18.0 %all-gather.3.cloned.1.call-done = bf16[1024,512]{1,0:T(8,128)(2,1)} async-done(((bf16[64,512]{1,0:T(8,128)(2,1)}), bf16[1024,512]{1,0:T(8,128)(2,1)}) %all-gather.3.cloned.1.call-update) | async-done | bytes 1048592 | tf_op jit(solution)/shard_map/all_gather | solution.py:69
  190.3 12.5 %fusion.14 = f32[1024,4864]{1,0:T(8,128)} fusion(bf16[1024,512]{1,0:T(8,128)(2,1)} %all-gather.3.cloned.1.call-done, bf16[512,4864]{1,0:T(8,128)(2,1)} %param.21), kind=kOutput, calls=%fused_computation.41 | convolution fusion | flops 5100273664 | bytes 25952256 | tf_op jit(solution)/shard_map/dot_general | solution.py:80
  202.9 0.6 copy-done.7
  203.5 25.1 %reduce-scatter.6.cloned.1.call-done = bf16[128,4864]{1,0:T(8,128)(2,1)} async-done(((bf16[1024,4864]{1,0:T(8,128)(2,1)}), bf16[128,4864]{1,0:T(8,128)(2,1)}) %reduce-scatter.6.cloned.1.call-update) | async-done | bytes 1245200 | tf_op jit(solution)/shard_map/reduce_scatter | solution.py:72
  228.5 1.5 reduce_max.24
  230.1 107.0 %reduce-scatter.4.cloned.1.call-done = f32[128,4864]{1,0:T(8,128)} async-done(((f32[1024,4864]{1,0:T(8,128)}), f32[128,4864]{1,0:T(8,128)}) %reduce-scatter.4.cloned.1.call-update) | async-done | bytes 2490384 | tf_op jit(solution)/shard_map/reduce_scatter | solution.py:79
  337.0 2.0 reduce_max.23
  339.1 41.3 %all-reduce.1 = (f32[128]{0:T(128)S(1)}, f32[128]{0:T(128)S(1)}) all-reduce(f32[128]{0:T(128)S(1)} %reduce_max.23, bf16[128]{0:T(256)(128)(2,1)S(1)} %reduce_max.24), channel_id=1, replica_groups=mesh['tok'=8,'voc'=16] {'voc'}, use_global_device_ids=true, to_apply=%region_2.3 | all-reduce | flops 256 | bytes 1792 | tf_op jit(solution)/shard_map/pmax | solution.py:92
  380.4 3.6 multiply_reduce_fusion
  384.0 35.5 %all-reduce = (f32[128]{0:T(128)S(1)}, f32[128]{0:T(128)S(1)}, f32[128]{0:T(128)S(1)}, f32[128]{0:T(128)S(1)}, f32[128]{0:T(128)S(1)}) all-reduce(f32[128]{0:T(128)S(1)} %get-tuple-element.5, f32[128]{0:T(128)S(1)} %get-tuple-element.4, f32[128]{0:T(128)S(1)} %get-tuple-element.3, ...), channel_id=1, replica_groups=mesh['tok'=8,'voc'=16] {'voc'}, use_global_device_ids=true, to_apply=%region_22.23 | all-reduce | flops 640 | bytes 5120 | tf_op jit(solution)/shard_map/psum | solution.py:94
  419.4 0.5 subtract_subtract_fusion
  420.0 3.5 multiply_convert_fusion
  423.6 51.8 %all-gather.5.cloned.1.call-done = bf16[1024,4864]{1,0:T(8,128)(2,1)} async-done(((bf16[128,4864]{1,0:T(8,128)(2,1)}), bf16[1024,4864]{1,0:T(8,128)(2,1)}) %all-gather.5.cloned.1.call-update) | async-done | bytes 9961488 | tf_op jit(solution)/shard_map/all_gather | solution.py:116
  475.4 11.1 %convolution_convert_fusion.3 = bf16[1024,512]{1,0:T(8,128)(2,1)} fusion(bf16[1024,4864]{1,0:T(8,128)(2,1)} %all-gather.5.cloned.1.call-done, bf16[512,4864]{1,0:T(8,128)(2,1)} %param.21), kind=kOutput, calls=%fused_computation.17 | convolution fusion | flops 5100797952 | bytes 15990784 | tf_op jit(solution)/shard_map/dot_general | solution.py:115
  486.5 74.6 %reduce-scatter.8.cloned.1.call-done = bf16[64,512]{1,0:T(8,128)(2,1)} async-done(((bf16[1024,512]{1,0:T(8,128)(2,1)}), bf16[64,512]{1,0:T(8,128)(2,1)}) %reduce-scatter.8.cloned.1.call-update) | async-done | bytes 65552 | tf_op jit(solution)/shard_map/reduce_scatter | solution.py:121
  (25 shorter events, 0.3 us)
Async XLA Ops:
  8.0 59.5 %copy-start = (bf16[384,4096]{1,0:T(8,128)(2,1)S(1)}, bf16[384,4096]{1,0:T(8,128)(2,1)}, u32[]{:S(2)}) copy-start(bf16[384,4096]{1,0:T(8,128)(2,1)} %param.17) | copy-start | bytes 9437188
  78.2 5.0 copy-start.4
  78.2 34.6 %all-to-all-start.1 = ((bf16[128,2,4096]{2,1,0:T(2,128)(2,1)}), bf16[128,2,4096]{2,1,0:T(2,128)(2,1)S(1)}, u32[]{:S(2)}, u32[]{:S(2)}) async-start(bf16[128,2,4096]{2,1,0:T(2,128)(2,1)} %reshape.61), calls=%async_computation.2 | async-start | bytes 4194304 | tf_op jit(solution)/shard_map/all_to_all | solution.py:57
  116.9 2.7 copy-start.3
  116.9 4.0 copy-start.5
  142.6 19.4 %all-to-all-start.3 = ((bf16[128,8,512]{2,0,1:T(8,128)(2,1)}), bf16[128,8,512]{2,0,1:T(8,128)(2,1)S(1)}, u32[]{:S(2)}, u32[]{:S(2)}) async-start(bf16[128,8,512]{2,0,1:T(8,128)(2,1)} %copy.16), calls=%async_computation.4 | async-start | bytes 2097152 | tf_op jit(solution)/shard_map/all_to_all | solution.py:68
  146.2 44.2 %all-gather.3.cloned.1.call-start = ((), (), s32[]{:S(2)}) async-start(), calls=%async_computation.7 | async-start | bytes 1114112 | tf_op jit(solution)/shard_map/all_gather | solution.py:69
  146.9 81.6 %reduce-scatter.6.cloned.1.call-start = ((), (), s32[]{:S(2)}) async-start(), calls=%async_computation.9 | async-start | bytes 11206656 | tf_op jit(solution)/shard_map/reduce_scatter | solution.py:72
  172.3 164.8 %reduce-scatter.4.cloned.1.call-start = ((), (), s32[]{:S(2)}) async-start(), calls=%async_computation.8 | async-start | bytes 22413312 | tf_op jit(solution)/shard_map/reduce_scatter | solution.py:79
  202.8 0.7 copy-start.7
  202.8 272.5 %all-gather.5.cloned.1.call-start = ((), (), s32[]{:S(2)}) async-start(), calls=%async_computation.10 | async-start | bytes 11206656 | tf_op jit(solution)/shard_map/all_gather | solution.py:116
  337.0 43.4 %copy-start.2 = (f32[128,4864]{1,0:T(8,128)S(1)}, f32[128,4864]{1,0:T(8,128)}, u32[]{:S(2)}) copy-start(f32[128,4864]{1,0:T(8,128)} %reduce-scatter.4.cloned.1.call-done) | copy-start | bytes 7471108
  339.1 80.9 %copy-start.6 = (f32[128]{0:T(128)S(1)}, f32[128]{0:T(128)}, u32[]{:S(2)}) copy-start(f32[128]{0:T(128)} %param.23) | copy-start | bytes 1540
  423.5 137.6 %reduce-scatter.8.cloned.1.call-start = ((), (), s32[]{:S(2)}) async-start(), calls=%async_computation.11 | async-start | bytes 1114112 | tf_op jit(solution)/shard_map/reduce_scatter | solution.py:121
  475.4 85.7 %copy-start.1 = (bf16[384,4096]{1,0:T(8,128)(2,1)S(1)}, bf16[384,4096]{1,0:T(8,128)(2,1)}, u32[]{:S(2)}) copy-start(bf16[384,4096]{1,0:T(8,128)(2,1)} %param.17) | copy-start | bytes 9437188
Sparse Core Ops, SparseCore 0:
  149.1 41.1 all-gather.2
  486.6 74.4 reduce-scatter.7
Sparse Core Ops, SparseCore 1:
  172.3 56.1 reduce-scatter.5
  230.9 106.1 reduce-scatter.3
  423.6 51.7 all-gather.4
